TPU v7x, 256 devices: a whole 4x4x8 slice. The times are simulated.
256 devices in a mesh: wide: 32 (over y, x, core), grp: 8 (over z).
Axes of the slice: x: 4, y: 4, z: 8, core: 2. Of those that a mesh axis runs over, the one named last changes fastest.
Arguments:
- solution: float32 [64, 262144], P(None, ('wide', 'grp')), may hold values from -6 to 6
- incident: float32 [64, 262144], P(None, ('wide', 'grp')), may hold values from -12 to 12
- leaf_blocks: float32 [512, 262144], P(None, ('wide', 'grp')), may hold values from -0.25 to 0.25
- leaf_inverse: float32 [512, 262144], P(None, ('wide', 'grp')), may hold values from -0.25 to 0.25
- col_basis: float32 [9, 96, 262144], P(None, None, ('wide', 'grp')), may hold values from -0.625 to 0.625
- row_basis: float32 [9, 96, 262144], P(None, None, ('wide', 'grp')), may hold values from -6 to 6
Outputs:
- refined: float32 [64, 262144], P(None, ('wide', 'grp'))
- residual: float32 [64, 262144], P(None, ('wide', 'grp'))
All inputs are finite; a program needn't handle non-finite values.
Results may differ from a plain program's by a relative error of at most 0.0001.
Values sent between devices are 32-bit elements; how exact they have to be, the bound alone decides.
A program may use at most 64 MiB of HBM per device.

v0:
```python
import jax
import jax.numpy as jnp
from jax import lax
from jax.sharding import PartitionSpec as P


def from_partner(block, axis, stride):
    count = lax.axis_size(axis)
    route = []
    for low in range(count):
        high = low | 1 << stride
        if high != low and high < count:
            route += [(low, high), (high, low)]
    return lax.ppermute(block, axis, route)


def leaf_apply(field, blocks):
    cols, rows = field.shape
    leaf = blocks.shape[0]
    count = rows // leaf
    pieces = field.reshape(cols, count, leaf)
    tables = blocks.reshape(leaf, count, leaf)
    image = jnp.einsum("pkj,jki->pki", pieces, tables, precision=lax.Precision.HIGHEST)
    return image.reshape(cols, rows)


def climb_tree(partials):
    grp_bits = lax.axis_size("grp").bit_length() - 1
    wide_bits = lax.axis_size("wide").bit_length() - 1
    gathered_coefs = []
    pending = partials
    for bit_pos in range(grp_bits):
        received = from_partner(pending, "grp", bit_pos)
        gathered_coefs.append(received[0])
        pending = (pending + received)[1:]
    for bit_pos in range(wide_bits):
        received = from_partner(pending, "wide", bit_pos)
        gathered_coefs.append(received[0])
        pending = (pending + received)[1:]
    return jnp.stack(gathered_coefs)


def operator(field, leaf_blocks, col_basis, row_basis):
    cols, rows = field.shape
    leaf = leaf_blocks.shape[0]
    image = leaf_apply(field, leaf_blocks)
    pieces = field.reshape(cols, 2, leaf)
    rights = row_basis[0].reshape(row_basis.shape[1], 2, leaf)
    lefts = col_basis[0].reshape(col_basis.shape[1], 2, leaf)
    leaf_coefs = jnp.einsum("pks,rks->kpr", pieces, rights, precision=lax.Precision.HIGHEST)[::-1]
    image = image + jnp.einsum(
        "kpr,rks->pks", leaf_coefs, lefts, precision=lax.Precision.HIGHEST
    ).reshape(cols, rows)
    partials = jnp.einsum("pn,lrn->lpr", field, row_basis[1:], precision=lax.Precision.HIGHEST)
    sibling_coefs = climb_tree(partials)
    image = image + jnp.einsum(
        "lpr,lrn->pn", sibling_coefs, col_basis[1:], precision=lax.Precision.HIGHEST
    )
    return image


def per_device(solution, incident, leaf_blocks, leaf_inverse, col_basis, row_basis):
    first_residual = incident - operator(solution, leaf_blocks, col_basis, row_basis)
    refined = solution + leaf_apply(first_residual, leaf_inverse)
    residual = incident - operator(refined, leaf_blocks, col_basis, row_basis)
    return (refined, residual)


def solution(mesh):
    in_specs = (
        P(None, ("wide", "grp")),
        P(None, ("wide", "grp")),
        P(None, ("wide", "grp")),
        P(None, ("wide", "grp")),
        P(None, None, ("wide", "grp")),
        P(None, None, ("wide", "grp")),
    )
    out_specs = (P(None, ("wide", "grp")), P(None, ("wide", "grp")))
    return jax.shard_map(
        per_device, mesh=mesh, in_specs=in_specs, out_specs=out_specs, check_vma=False
    )
```

profile of v0, /device:TPU:16, one launch (start us, length us, event | category | flops | bytes accessed | tf_op | source)
XLA Modules:
  0.0 137.6 jit_solution(9455229727896869346)
XLA Ops:
  0.7 5.6 %convolution_bitcast_fusion.1 = f32[8,64,96]{2,1,0:T(8,128)S(1)} fusion(f32[9,96,1024]{2,1,0:T(8,128)} %param.11, f32[64,1024]{1,0:T(8,128)} %param.6), kind=kOutput, calls=%fused_computation.25 | convolution fusion | flops 603979776 | bytes 3997696 | tf_op jit(solution)/shard_map/pn,lrn->lpr/dot_general | solution.py:54
  6.3 2.0 %collective-permute-start = (f32[8,64,96]{2,1,0:T(8,128)S(1)}, f32[8,64,96]{2,1,0:T(8,128)S(1)}, u32[]{:S(2)}, u32[]{:S(2)}) collective-permute-start(f32[8,64,96]{2,1,0:T(8,128)S(1)} %convolution_bitcast_fusion.1), channel_id=1, source_target_pairs={{0,1},{1,0},{2,3},{3,2},{4,5},{5,4},{6,7},{7,6},{8,9},{9,8},{10,11... | collective-permute-start | bytes 589832 | tf_op jit(solution)/shard_map/ppermute | solution.py:14
  8.3 0.3 reshape_squeeze.9
  8.6 0.3 reshape_squeeze.8
  9.0 0.6 fusion.56
  9.6 0.5 convolution_bitcast_fusion
  10.0 4.5 %collective-permute-done = f32[8,64,96]{2,1,0:T(8,128)S(1)} collective-permute-done((f32[8,64,96]{2,1,0:T(8,128)S(1)}, f32[8,64,96]{2,1,0:T(8,128)S(1)}, u32[]{:S(2)}, u32[]{:S(2)}) %collective-permute-start) | collective-permute-done | bytes 196640 | tf_op jit(solution)/shard_map/ppermute | solution.py:14
  14.6 0.7 copy-done.13
  15.3 3.4 %collective-permute-start.1 = (f32[7,64,96]{2,1,0:T(8,128)S(1)}, f32[7,64,96]{2,1,0:T(8,128)S(1)}, u32[]{:S(2)}, u32[]{:S(2)}) collective-permute-start(f32[7,64,96]{2,1,0:T(8,128)S(1)} %slice_add_fusion.1), channel_id=1, source_target_pairs={{0,2},{2,0},{1,3},{3,1},{4,6},{6,4},{5,7},{7,5},{8,10},{10,8},{9,1... | collective-permute-start | bytes 516104 | tf_op jit(solution)/shard_map/ppermute | solution.py:14
  18.7 0.8 constant_dynamic-update-slice_fusion.7
  19.5 9.1 %collective-permute-done.1 = f32[7,64,96]{2,1,0:T(8,128)S(1)} collective-permute-done((f32[7,64,96]{2,1,0:T(8,128)S(1)}, f32[7,64,96]{2,1,0:T(8,128)S(1)}, u32[]{:S(2)}, u32[]{:S(2)}) %collective-permute-start.1) | collective-permute-done | bytes 172064 | tf_op jit(solution)/shard_map/ppermute | solution.py:14
  28.6 6.3 %collective-permute-start.2 = (f32[6,64,96]{2,1,0:T(8,128)S(1)}, f32[6,64,96]{2,1,0:T(8,128)S(1)}, u32[]{:S(2)}, u32[]{:S(2)}) collective-permute-start(f32[6,64,96]{2,1,0:T(8,128)S(1)} %slice_add_fusion.3), channel_id=1, source_target_pairs={{0,4},{4,0},{1,5},{5,1},{2,6},{6,2},{3,7},{7,3},{8,12},{12,8},{9,1... | collective-permute-start | bytes 442376 | tf_op jit(solution)/shard_map/ppermute | solution.py:14
  34.9 7.6 %collective-permute-done.2 = f32[6,64,96]{2,1,0:T(8,128)S(1)} collective-permute-done((f32[6,64,96]{2,1,0:T(8,128)S(1)}, f32[6,64,96]{2,1,0:T(8,128)S(1)}, u32[]{:S(2)}, u32[]{:S(2)}) %collective-permute-start.2) | collective-permute-done | bytes 147488 | tf_op jit(solution)/shard_map/ppermute | solution.py:14
  42.5 0.1 collective-permute-start.3
  42.6 1.4 collective-permute-done.3
  44.0 1.6 %collective-permute-start.4 = (f32[4,64,96]{2,1,0:T(8,128)S(1)}, f32[4,64,96]{2,1,0:T(8,128)S(1)}, u32[]{:S(2)}, u32[]{:S(2)}) collective-permute-start(f32[4,64,96]{2,1,0:T(8,128)S(1)} %slice_add_fusion.7), channel_id=1, source_target_pairs={{0,16},{16,0},{8,24},{24,8},{32,48},{48,32},{40,56},{56,40},{64,80... | collective-permute-start | bytes 294920 | tf_op jit(solution)/shard_map/ppermute | solution.py:14
  45.6 4.0 %collective-permute-done.4 = f32[4,64,96]{2,1,0:T(8,128)S(1)} collective-permute-done((f32[4,64,96]{2,1,0:T(8,128)S(1)}, f32[4,64,96]{2,1,0:T(8,128)S(1)}, u32[]{:S(2)}, u32[]{:S(2)}) %collective-permute-start.4) | collective-permute-done | bytes 98336 | tf_op jit(solution)/shard_map/ppermute | solution.py:14
  49.6 3.1 %collective-permute-start.5 = (f32[3,64,96]{2,1,0:T(8,128)S(1)}, f32[3,64,96]{2,1,0:T(8,128)S(1)}, u32[]{:S(2)}, u32[]{:S(2)}) collective-permute-start(f32[3,64,96]{2,1,0:T(8,128)S(1)} %slice_add_fusion.9), channel_id=1, source_target_pairs={{0,32},{32,0},{8,40},{40,8},{16,48},{48,16},{24,56},{56,24},{64,96... | collective-permute-start | bytes 221192 | tf_op jit(solution)/shard_map/ppermute | solution.py:14
  52.7 3.1 %collective-permute-done.5 = f32[3,64,96]{2,1,0:T(8,128)S(1)} collective-permute-done((f32[3,64,96]{2,1,0:T(8,128)S(1)}, f32[3,64,96]{2,1,0:T(8,128)S(1)}, u32[]{:S(2)}, u32[]{:S(2)}) %collective-permute-start.5) | collective-permute-done | bytes 73760 | tf_op jit(solution)/shard_map/ppermute | solution.py:14
  55.8 1.4 collective-permute-start.6
  57.2 3.0 %collective-permute-done.6 = f32[2,64,96]{2,1,0:T(8,128)S(1)} collective-permute-done((f32[2,64,96]{2,1,0:T(8,128)S(1)}, f32[2,64,96]{2,1,0:T(8,128)S(1)}, u32[]{:S(2)}, u32[]{:S(2)}) %collective-permute-start.6) | collective-permute-done | bytes 49184 | tf_op jit(solution)/shard_map/ppermute | solution.py:14
  60.2 0.6 collective-permute-start.7
  60.8 3.2 %fusion.21 = f32[2,8,8,512]{3,2,1,0:T(8,128)S(1)} fusion(f32[64,2,512]{2,0,1:T(8,128)S(1)} %convolution_bitcast_fusion, f32[64,2,8,512]{3,2,1,0:T(8,128)} %bitcast.84, f32[8,2,8,512]{3,2,1,0:T(8,128)} %bitcast.88), kind=kOutput, calls=%fused_computation.17 | convolution fusion | flops 402718720 | bytes 2883584 | tf_op jit(solution)/shard_map/pkj,jki->pki/dot_general | solution.py:23
  64.0 1.8 %collective-permute-done.7 = f32[1,64,96]{2,1,0:T(8,128)S(1)} collective-permute-done((f32[1,64,96]{2,1,0:T(8,128)S(1)}, f32[1,64,96]{2,1,0:T(8,128)S(1)}, u32[]{:S(2)}, u32[]{:S(2)}) %collective-permute-start.7) | collective-permute-done | bytes 24608 | tf_op jit(solution)/shard_map/ppermute | solution.py:14
  65.9 2.4 %fusion.51 = f32[64,1024]{1,0:T(8,128)S(1)} fusion(f32[64,1024]{1,0:T(8,128)S(1)} %copy-done.11, f32[64,1024]{1,0:T(8,128)S(1)} %bitcast.92, f32[8,64,96]{2,1,0:T(8,128)S(1)} %constant_dynamic-update-slice_fusion, f32[9,96,1024]{2,1,0:T(8,128)S(1)} %copy-done.1), kind=kOutput, calls=%fused_computation.29 | convolution fusion | flops 604110848 | bytes 4194304 | tf_op jit(solution)/shard_map/lpr,lrn->pn/dot_general | solution.py:56
  68.3 1.4 %fusion.30 = f32[2,8,8,512]{3,2,1,0:T(8,128)S(1)} fusion(f32[64,2,8,512]{3,2,1,0:T(8,128)S(1)} %bitcast.90, f32[8,2,8,512]{3,2,1,0:T(8,128)S(1)} %bitcast.91), kind=kOutput, calls=%fused_computation.20 | convolution fusion | flops 402653184 | bytes 2621440 | tf_op jit(solution)/shard_map/pkj,jki->pki/dot_general | solution.py:23
  69.8 4.4 %fusion.39 = f32[8,64,96]{2,1,0:T(8,128)} fusion(f32[9,96,1024]{2,1,0:T(8,128)S(1)} %copy-done, f32[64,1024]{1,0:T(8,128)S(1)} %add.76), kind=kOutput, calls=%fused_computation.24 | convolution fusion | flops 603979776 | bytes 3604480 | tf_op jit(solution)/shard_map/pn,lrn->lpr/dot_general | solution.py:54
  74.2 1.2 fusion.54
  75.4 1.5 %rev.7 = f32[2,64,96]{2,1,0:T(8,128)} reverse(f32[2,64,96]{2,1,0:T(8,128)} %fusion.54), dimensions={0} | reverse | bytes 98304 | tf_op jit(solution)/shard_map/rev | solution.py:50
  76.9 1.6 %fusion.58 = f32[2,64,512]{2,1,0:T(8,128)S(1)} fusion(f32[2,64,96]{2,1,0:T(8,128)} %rev.7, f32[96,2,512]{2,1,0:T(2,128)} %copy-done.7), kind=kOutput, calls=%fused_computation.34 | convolution fusion | flops 75497472 | bytes 704512 | tf_op jit(solution)/shard_map/kpr,rks->pks/dot_general | solution.py:51
  78.5 4.9 %collective-permute-done.8 = f32[8,64,96]{2,1,0:T(8,128)S(1)} collective-permute-done((f32[8,64,96]{2,1,0:T(8,128)}, f32[8,64,96]{2,1,0:T(8,128)S(1)}, u32[]{:S(2)}, u32[]{:S(2)}) %collective-permute-start.8) | collective-permute-done | bytes 196640 | tf_op jit(solution)/shard_map/ppermute | solution.py:14
  83.5 1.0 slice_add_fusion
  84.4 4.7 %collective-permute-start.9 = (f32[7,64,96]{2,1,0:T(8,128)S(1)}, f32[7,64,96]{2,1,0:T(8,128)S(1)}, u32[]{:S(2)}, u32[]{:S(2)}) collective-permute-start(f32[7,64,96]{2,1,0:T(8,128)S(1)} %slice_add_fusion), channel_id=1, source_target_pairs={{0,2},{2,0},{1,3},{3,1},{4,6},{6,4},{5,7},{7,5},{8,10},{10,8},{9,1... | collective-permute-start | bytes 516104 | tf_op jit(solution)/shard_map/ppermute | solution.py:14
  89.1 9.7 %collective-permute-done.9 = f32[7,64,96]{2,1,0:T(8,128)S(1)} collective-permute-done((f32[7,64,96]{2,1,0:T(8,128)S(1)}, f32[7,64,96]{2,1,0:T(8,128)S(1)}, u32[]{:S(2)}, u32[]{:S(2)}) %collective-permute-start.9) | collective-permute-done | bytes 172064 | tf_op jit(solution)/shard_map/ppermute | solution.py:14
  98.8 2.8 %collective-permute-start.10 = (f32[6,64,96]{2,1,0:T(8,128)S(1)}, f32[6,64,96]{2,1,0:T(8,128)S(1)}, u32[]{:S(2)}, u32[]{:S(2)}) collective-permute-start(f32[6,64,96]{2,1,0:T(8,128)S(1)} %slice_add_fusion.2), channel_id=1, source_target_pairs={{0,4},{4,0},{1,5},{5,1},{2,6},{6,2},{3,7},{7,3},{8,12},{12,8},{9,1... | collective-permute-start | bytes 442376 | tf_op jit(solution)/shard_map/ppermute | solution.py:14
  101.6 9.0 %collective-permute-done.10 = f32[6,64,96]{2,1,0:T(8,128)S(1)} collective-permute-done((f32[6,64,96]{2,1,0:T(8,128)S(1)}, f32[6,64,96]{2,1,0:T(8,128)S(1)}, u32[]{:S(2)}, u32[]{:S(2)}) %collective-permute-start.10) | collective-permute-done | bytes 147488 | tf_op jit(solution)/shard_map/ppermute | solution.py:14
  110.6 0.1 collective-permute-start.11
  110.8 1.4 collective-permute-done.11
  112.1 1.6 %collective-permute-start.12 = (f32[4,64,96]{2,1,0:T(8,128)S(1)}, f32[4,64,96]{2,1,0:T(8,128)S(1)}, u32[]{:S(2)}, u32[]{:S(2)}) collective-permute-start(f32[4,64,96]{2,1,0:T(8,128)S(1)} %slice_add_fusion.6), channel_id=1, source_target_pairs={{0,16},{16,0},{8,24},{24,8},{32,48},{48,32},{40,56},{56,40},{64,80... | collective-permute-start | bytes 294920 | tf_op jit(solution)/shard_map/ppermute | solution.py:14
  113.7 4.1 %collective-permute-done.12 = f32[4,64,96]{2,1,0:T(8,128)S(1)} collective-permute-done((f32[4,64,96]{2,1,0:T(8,128)S(1)}, f32[4,64,96]{2,1,0:T(8,128)S(1)}, u32[]{:S(2)}, u32[]{:S(2)}) %collective-permute-start.12) | collective-permute-done | bytes 98336 | tf_op jit(solution)/shard_map/ppermute | solution.py:14
  117.8 3.1 %collective-permute-start.13 = (f32[3,64,96]{2,1,0:T(8,128)S(1)}, f32[3,64,96]{2,1,0:T(8,128)S(1)}, u32[]{:S(2)}, u32[]{:S(2)}) collective-permute-start(f32[3,64,96]{2,1,0:T(8,128)S(1)} %slice_add_fusion.8), channel_id=1, source_target_pairs={{0,32},{32,0},{8,40},{40,8},{16,48},{48,16},{24,56},{56,24},{64,96... | collective-permute-start | bytes 221192 | tf_op jit(solution)/shard_map/ppermute | solution.py:14
  120.9 3.1 %collective-permute-done.13 = f32[3,64,96]{2,1,0:T(8,128)S(1)} collective-permute-done((f32[3,64,96]{2,1,0:T(8,128)S(1)}, f32[3,64,96]{2,1,0:T(8,128)S(1)}, u32[]{:S(2)}, u32[]{:S(2)}) %collective-permute-start.13) | collective-permute-done | bytes 73760 | tf_op jit(solution)/shard_map/ppermute | solution.py:14
  124.0 1.4 collective-permute-start.14
  125.4 3.3 %collective-permute-done.14 = f32[2,64,96]{2,1,0:T(8,128)S(1)} collective-permute-done((f32[2,64,96]{2,1,0:T(8,128)S(1)}, f32[2,64,96]{2,1,0:T(8,128)S(1)}, u32[]{:S(2)}, u32[]{:S(2)}) %collective-permute-start.14) | collective-permute-done | bytes 49184 | tf_op jit(solution)/shard_map/ppermute | solution.py:14
  128.7 0.3 collective-permute-start.15
  129.1 1.4 fusion.27
  130.5 4.0 %collective-permute-done.15 = f32[1,64,96]{2,1,0:T(8,128)S(1)} collective-permute-done((f32[1,64,96]{2,1,0:T(8,128)S(1)}, f32[1,64,96]{2,1,0:T(8,128)S(1)}, u32[]{:S(2)}, u32[]{:S(2)}) %collective-permute-start.15) | collective-permute-done | bytes 24608 | tf_op jit(solution)/shard_map/ppermute | solution.py:14
  134.5 3.1 %fusion.45 = f32[64,1024]{1,0:T(8,128)} fusion(f32[64,1024]{1,0:T(8,128)S(1)} %copy-done.12, f32[64,1024]{1,0:T(8,128)S(1)} %bitcast.93, f32[8,64,96]{2,1,0:T(8,128)S(1)} %constant_dynamic-update-slice_fusion.8, f32[9,96,1024]{2,1,0:T(8,128)S(1)} %copy-done.1), kind=kOutput, calls=%fused_computation.27 | convolution fusion | flops 604110848 | bytes 4194304 | tf_op jit(solution)/shard_map/lpr,lrn->pn/dot_general | solution.py:56
  (63 shorter events, 0.5 us)
Async XLA Ops:
  0.6 8.0 %slice-start = ((f32[9,96,1024]{2,1,0:T(8,128)}), f32[1,96,1024]{2,1,0:T(8,128)S(1)}, s32[]{:S(2)}) async-start(f32[9,96,1024]{2,1,0:T(8,128)} %param.11), calls=%async_computation | async-start | bytes 786432 | tf_op jit(solution)/shard_map/slice | solution.py:48
  0.6 8.3 %copy-start.5 = (f32[64,1024]{1,0:T(8,128)S(1)}, f32[64,1024]{1,0:T(8,128)}, u32[]{:S(2)}) copy-start(f32[64,1024]{1,0:T(8,128)} %param.6) | copy-start | bytes 786436
  0.7 7.6 %slice-start.1 = ((f32[9,96,1024]{2,1,0:T(8,128)}), f32[1,96,1024]{2,1,0:T(8,128)S(1)}, s32[]{:S(2)}) async-start(f32[9,96,1024]{2,1,0:T(8,128)} %param.10), calls=%async_computation.1 | async-start | bytes 786432 | tf_op jit(solution)/shard_map/slice | solution.py:49
  6.3 8.3 %collective-permute-start = (f32[8,64,96]{2,1,0:T(8,128)S(1)}, f32[8,64,96]{2,1,0:T(8,128)S(1)}, u32[]{:S(2)}, u32[]{:S(2)}) collective-permute-start(f32[8,64,96]{2,1,0:T(8,128)S(1)} %convolution_bitcast_fusion.1), channel_id=1, source_target_pairs={{0,1},{1,0},{2,3},{3,2},{4,5},{5,4},{6,7},{7,6},{8,9},{9,8},{10,11... | collective-permute-start | bytes 589832 | tf_op jit(solution)/shard_map/ppermute | solution.py:14
  8.6 6.0 %copy-start.7 = (f32[96,2,512]{2,1,0:T(2,128)}, f32[96,2,512]{2,1,0:T(2,128)S(1)}, u32[]{:S(2)}) copy-start(f32[96,2,512]{2,1,0:T(2,128)S(1)} %reshape_squeeze.9) | copy-start | bytes 1179652
  9.0 5.6 %copy-start.8 = (f32[96,2,512]{2,1,0:T(2,128)}, f32[96,2,512]{2,1,0:T(2,128)S(1)}, u32[]{:S(2)}) copy-start(f32[96,2,512]{2,1,0:T(2,128)S(1)} %reshape_squeeze.8) | copy-start | bytes 1179652
  14.6 0.7 copy-start.13
  15.3 50.6 %copy-start.1 = (f32[9,96,1024]{2,1,0:T(8,128)S(1)}, f32[9,96,1024]{2,1,0:T(8,128)}, u32[]{:S(2)}) copy-start(f32[9,96,1024]{2,1,0:T(8,128)} %param.10) | copy-start | bytes 10616836
  15.3 50.6 %copy-start.11 = (f32[64,1024]{1,0:T(8,128)S(1)}, f32[64,1024]{1,0:T(8,128)}, u32[]{:S(2)}) copy-start(f32[64,1024]{1,0:T(8,128)} %param.7) | copy-start | bytes 786436
  15.3 13.2 %collective-permute-start.1 = (f32[7,64,96]{2,1,0:T(8,128)S(1)}, f32[7,64,96]{2,1,0:T(8,128)S(1)}, u32[]{:S(2)}, u32[]{:S(2)}) collective-permute-start(f32[7,64,96]{2,1,0:T(8,128)S(1)} %slice_add_fusion.1), channel_id=1, source_target_pairs={{0,2},{2,0},{1,3},{3,1},{4,6},{6,4},{5,7},{7,5},{8,10},{10,8},{9,1... | collective-permute-start | bytes 516104 | tf_op jit(solution)/shard_map/ppermute | solution.py:14
  28.6 13.9 %collective-permute-start.2 = (f32[6,64,96]{2,1,0:T(8,128)S(1)}, f32[6,64,96]{2,1,0:T(8,128)S(1)}, u32[]{:S(2)}, u32[]{:S(2)}) collective-permute-start(f32[6,64,96]{2,1,0:T(8,128)S(1)} %slice_add_fusion.3), channel_id=1, source_target_pairs={{0,4},{4,0},{1,5},{5,1},{2,6},{6,2},{3,7},{7,3},{8,12},{12,8},{9,1... | collective-permute-start | bytes 442376 | tf_op jit(solution)/shard_map/ppermute | solution.py:14
  42.5 1.5 %collective-permute-start.3 = (f32[5,64,96]{2,1,0:T(8,128)S(1)}, f32[5,64,96]{2,1,0:T(8,128)S(1)}, u32[]{:S(2)}, u32[]{:S(2)}) collective-permute-start(f32[5,64,96]{2,1,0:T(8,128)S(1)} %slice_add_fusion.5), channel_id=1, source_target_pairs={{0,8},{8,0},{16,24},{24,16},{32,40},{40,32},{48,56},{56,48},{64,72... | collective-permute-start | bytes 368648 | tf_op jit(solution)/shard_map/ppermute | solution.py:14
  44.0 5.6 %collective-permute-start.4 = (f32[4,64,96]{2,1,0:T(8,128)S(1)}, f32[4,64,96]{2,1,0:T(8,128)S(1)}, u32[]{:S(2)}, u32[]{:S(2)}) collective-permute-start(f32[4,64,96]{2,1,0:T(8,128)S(1)} %slice_add_fusion.7), channel_id=1, source_target_pairs={{0,16},{16,0},{8,24},{24,8},{32,48},{48,32},{40,56},{56,40},{64,80... | collective-permute-start | bytes 294920 | tf_op jit(solution)/shard_map/ppermute | solution.py:14
  49.6 6.2 %collective-permute-start.5 = (f32[3,64,96]{2,1,0:T(8,128)S(1)}, f32[3,64,96]{2,1,0:T(8,128)S(1)}, u32[]{:S(2)}, u32[]{:S(2)}) collective-permute-start(f32[3,64,96]{2,1,0:T(8,128)S(1)} %slice_add_fusion.9), channel_id=1, source_target_pairs={{0,32},{32,0},{8,40},{40,8},{16,48},{48,16},{24,56},{56,24},{64,96... | collective-permute-start | bytes 221192 | tf_op jit(solution)/shard_map/ppermute | solution.py:14
  55.8 4.4 %collective-permute-start.6 = (f32[2,64,96]{2,1,0:T(8,128)S(1)}, f32[2,64,96]{2,1,0:T(8,128)S(1)}, u32[]{:S(2)}, u32[]{:S(2)}) collective-permute-start(f32[2,64,96]{2,1,0:T(8,128)S(1)} %slice_add_fusion.11), channel_id=1, source_target_pairs={{0,64},{64,0},{8,72},{72,8},{16,80},{80,16},{24,88},{88,24},{32,96... | collective-permute-start | bytes 147464 | tf_op jit(solution)/shard_map/ppermute | solution.py:14
  60.2 5.7 %collective-permute-start.7 = (f32[1,64,96]{2,1,0:T(8,128)S(1)}, f32[1,64,96]{2,1,0:T(8,128)S(1)}, u32[]{:S(2)}, u32[]{:S(2)}) collective-permute-start(f32[1,64,96]{2,1,0:T(8,128)S(1)} %get-tuple-element.4), channel_id=1, source_target_pairs={{0,128},{128,0},{8,136},{136,8},{16,144},{144,16},{24,152},{152,24... | collective-permute-start | bytes 73736 | tf_op jit(solution)/shard_map/ppermute | solution.py:14
  60.8 7.5 %copy-start.10 = (f32[512,1024]{1,0:T(8,128)S(1)}, f32[512,1024]{1,0:T(8,128)}, u32[]{:S(2)}) copy-start(f32[512,1024]{1,0:T(8,128)} %param.9) | copy-start | bytes 6291460
  65.9 3.9 %copy-start.6 = (f32[64,1024]{1,0:T(8,128)S(1)}, f32[64,1024]{1,0:T(8,128)}, u32[]{:S(2)}) copy-start(f32[64,1024]{1,0:T(8,128)} %param.6) | copy-start | bytes 786436
  65.9 3.9 %copy-start = (f32[9,96,1024]{2,1,0:T(8,128)S(1)}, f32[9,96,1024]{2,1,0:T(8,128)}, u32[]{:S(2)}) copy-start(f32[9,96,1024]{2,1,0:T(8,128)} %param.11) | copy-start | bytes 10616836
  69.7 4.5 %copy-start.9 = (f32[96,2,512]{2,1,0:T(2,128)S(1)}, f32[96,2,512]{2,1,0:T(2,128)}, u32[]{:S(2)}) copy-start(f32[96,2,512]{2,1,0:T(2,128)} %copy-done.8) | copy-start | bytes 1179652
  69.8 4.4 %copy-start.3 = (f32[64,1024]{1,0:T(8,128)}, f32[64,1024]{1,0:T(8,128)S(1)}, u32[]{:S(2)}) copy-start(f32[64,1024]{1,0:T(8,128)S(1)} %add.76) | copy-start | bytes 786436
  76.9 52.2 %copy-start.2 = (f32[512,1024]{1,0:T(8,128)S(1)}, f32[512,1024]{1,0:T(8,128)}, u32[]{:S(2)}) copy-start(f32[512,1024]{1,0:T(8,128)} %param.8) | copy-start | bytes 6291460
  76.9 52.2 %copy-start.4 = (f32[64,1024]{1,0:T(8,128)S(1)}, f32[64,1024]{1,0:T(8,128)}, u32[]{:S(2)}) copy-start(f32[64,1024]{1,0:T(8,128)} %copy-done.3) | copy-start | bytes 786436
  76.9 6.6 %collective-permute-start.8 = (f32[8,64,96]{2,1,0:T(8,128)}, f32[8,64,96]{2,1,0:T(8,128)S(1)}, u32[]{:S(2)}, u32[]{:S(2)}) collective-permute-start(f32[8,64,96]{2,1,0:T(8,128)} %fusion.39), channel_id=1, source_target_pairs={{0,1},{1,0},{2,3},{3,2},{4,5},{5,4},{6,7},{7,6},{8,9},{9,8},{10,11... | collective-permute-start | bytes 589832 | tf_op jit(solution)/shard_map/ppermute | solution.py:14
  84.4 50.0 %copy-start.12 = (f32[64,1024]{1,0:T(8,128)S(1)}, f32[64,1024]{1,0:T(8,128)}, u32[]{:S(2)}) copy-start(f32[64,1024]{1,0:T(8,128)} %param.7) | copy-start | bytes 786436
  84.4 14.4 %collective-permute-start.9 = (f32[7,64,96]{2,1,0:T(8,128)S(1)}, f32[7,64,96]{2,1,0:T(8,128)S(1)}, u32[]{:S(2)}, u32[]{:S(2)}) collective-permute-start(f32[7,64,96]{2,1,0:T(8,128)S(1)} %slice_add_fusion), channel_id=1, source_target_pairs={{0,2},{2,0},{1,3},{3,1},{4,6},{6,4},{5,7},{7,5},{8,10},{10,8},{9,1... | collective-permute-start | bytes 516104 | tf_op jit(solution)/shard_map/ppermute | solution.py:14
  98.8 11.8 %collective-permute-start.10 = (f32[6,64,96]{2,1,0:T(8,128)S(1)}, f32[6,64,96]{2,1,0:T(8,128)S(1)}, u32[]{:S(2)}, u32[]{:S(2)}) collective-permute-start(f32[6,64,96]{2,1,0:T(8,128)S(1)} %slice_add_fusion.2), channel_id=1, source_target_pairs={{0,4},{4,0},{1,5},{5,1},{2,6},{6,2},{3,7},{7,3},{8,12},{12,8},{9,1... | collective-permute-start | bytes 442376 | tf_op jit(solution)/shard_map/ppermute | solution.py:14
  110.6 1.5 %collective-permute-start.11 = (f32[5,64,96]{2,1,0:T(8,128)S(1)}, f32[5,64,96]{2,1,0:T(8,128)S(1)}, u32[]{:S(2)}, u32[]{:S(2)}) collective-permute-start(f32[5,64,96]{2,1,0:T(8,128)S(1)} %slice_add_fusion.4), channel_id=1, source_target_pairs={{0,8},{8,0},{16,24},{24,16},{32,40},{40,32},{48,56},{56,48},{64,72... | collective-permute-start | bytes 368648 | tf_op jit(solution)/shard_map/ppermute | solution.py:14
  112.1 5.6 %collective-permute-start.12 = (f32[4,64,96]{2,1,0:T(8,128)S(1)}, f32[4,64,96]{2,1,0:T(8,128)S(1)}, u32[]{:S(2)}, u32[]{:S(2)}) collective-permute-start(f32[4,64,96]{2,1,0:T(8,128)S(1)} %slice_add_fusion.6), channel_id=1, source_target_pairs={{0,16},{16,0},{8,24},{24,8},{32,48},{48,32},{40,56},{56,40},{64,80... | collective-permute-start | bytes 294920 | tf_op jit(solution)/shard_map/ppermute | solution.py:14
  117.8 6.2 %collective-permute-start.13 = (f32[3,64,96]{2,1,0:T(8,128)S(1)}, f32[3,64,96]{2,1,0:T(8,128)S(1)}, u32[]{:S(2)}, u32[]{:S(2)}) collective-permute-start(f32[3,64,96]{2,1,0:T(8,128)S(1)} %slice_add_fusion.8), channel_id=1, source_target_pairs={{0,32},{32,0},{8,40},{40,8},{16,48},{48,16},{24,56},{56,24},{64,96... | collective-permute-start | bytes 221192 | tf_op jit(solution)/shard_map/ppermute | solution.py:14
  124.0 4.7 %collective-permute-start.14 = (f32[2,64,96]{2,1,0:T(8,128)S(1)}, f32[2,64,96]{2,1,0:T(8,128)S(1)}, u32[]{:S(2)}, u32[]{:S(2)}) collective-permute-start(f32[2,64,96]{2,1,0:T(8,128)S(1)} %slice_add_fusion.10), channel_id=1, source_target_pairs={{0,64},{64,0},{8,72},{72,8},{16,80},{80,16},{24,88},{88,24},{32,96... | collective-permute-start | bytes 147464 | tf_op jit(solution)/shard_map/ppermute | solution.py:14
  128.7 5.7 %collective-permute-start.15 = (f32[1,64,96]{2,1,0:T(8,128)S(1)}, f32[1,64,96]{2,1,0:T(8,128)S(1)}, u32[]{:S(2)}, u32[]{:S(2)}) collective-permute-start(f32[1,64,96]{2,1,0:T(8,128)S(1)} %get-tuple-element.2), channel_id=1, source_target_pairs={{0,128},{128,0},{8,136},{136,8},{16,144},{144,16},{24,152},{152,24... | collective-permute-start | bytes 73736 | tf_op jit(solution)/shard_map/ppermute | solution.py:14
where the time goes:
time: 138 us
  waiting for transfers between devices  74 us (54%)
  starting transfers between devices  32.3 us (23%)
  matrix products  25.3 us (18%)
  local copies, waits for them, and re-layouts  3.79 us (3%)
    ppermute x16, waiting for transfers between devices, from_partner(): return lax.ppermute(block, axis, route)  74 us
    ppermute x16, starting transfers between devices, from_partner(): return lax.ppermute(block, axis, route)  32.3 us
    dot_general x2, matrix products, operator(): jnp.einsum('pn,lrn->lpr', field, row_basis[1:], precision=lax.Precision.H...  9.97 us
    dot_general x3, matrix products, leaf_apply(): jnp.einsum('pkj,jki->pki', pieces, tables, precision=lax.Precision.HIGHEST)  5.93 us
    dot_general x2, matrix products, operator(): jnp.einsum('lpr,lrn->pn', sibling_coefs, col_basis[1:], precision=lax.Pre...  5.53 us
  transfers between devices with their start and end apart: 16, of which 16 were waited for; matrix products, arithmetic and copies ran while one was open for 6% of the time, Pallas kernels for 0%

commit v1 on v0

v1 whole, which is shorter than its diff:
```python
import functools

import jax
import jax.numpy as jnp
from jax import lax
from jax.experimental import pallas as pl
from jax.experimental.pallas import tpu as pltpu
from jax.sharding import PartitionSpec as P

MESH = pl.DeviceIdType.MESH
F32 = jnp.float32
BF16 = jnp.bfloat16
RANK = 96
COLS = 64
ROWS = 1024
LEAF = 512
HALF = 384
NEAR = (1, 2, 3, 4)
FAR = (8, 5, 6, 7)
FAR_LANE = {level: RANK * i for i, level in enumerate(FAR)}


def flip(value, mask):
    for bit in range(4):
        if mask >> bit & 1:
            value = value + (1 - 2 * ((value // (1 << bit)) % 2)) * (1 << bit)
    return value


def level_of(mask):
    return 5 + mask.bit_length() - 1


def tiles_of(level):
    low = FAR_LANE[level]
    return low // 128, (low + RANK - 1) // 128 + 1


def split(value):
    high = value.astype(BF16)
    low = (value - high.astype(F32)).astype(BF16)
    return high, low


def split_rows(src, high_ref, low_ref, step=32):
    @pl.loop(0, src.shape[0] // step)
    def _(i):
        rows = pl.ds(pl.multiple_of(i * step, step), step)
        high, low = split(src[rows, :])
        high_ref[rows, :] = high
        low_ref[rows, :] = low


def stack_split(value):
    high, low = split(value)
    return jnp.concatenate([high, low], axis=0)


def mul(stacked, high, low):
    top = jnp.dot(stacked, high, preferred_element_type=F32)
    return top[:COLS] + top[COLS:] + jnp.dot(stacked[:COLS], low, preferred_element_type=F32)


def mul_t(stacked, high, low):
    dims = (((1,), (1,)), ((), ()))
    top = lax.dot_general(stacked, high, dims, preferred_element_type=F32)
    return top[:COLS] + top[COLS:] + lax.dot_general(stacked[:COLS], low, dims, preferred_element_type=F32)


def kernel(sol_hbm, inc_hbm, leaf_hbm, inv_hbm, col_hbm, row_hbm, ref_hbm, res_hbm, *scratch):
    (sol, inc, leaf, inv, colf, rowf, col0, row0,
     leaf_h, leaf_l, inv_h, inv_l, col_h, col_l, row_h, row_l, col0_h, col0_l, row0_h, row0_l,
     base, refined, out,
     near, far, swap, mine, ring_far, sum_far, cross, fin_far, all_far,
     ring_near, fin_near, fin_four, all_near, all_four,
     in_sem, out_sem, send_sem, recv_sem) = scratch

    wide = lax.axis_index("wide")
    z = lax.axis_index("grp")
    core = wide % 2
    plane = wide // 2
    other = wide + 1 - 2 * core

    loads = {}

    def load(name, src, dst):
        copy = pltpu.make_async_copy(src, dst, in_sem.at[len(loads)])
        copy.start()
        loads[name] = copy

    load("sol", sol_hbm, sol)
    for i, level in enumerate(FAR):
        load(("row", i + 4), row_hbm.at[level], rowf.at[pl.ds(HALF + RANK * i, RANK)])
    for i, level in enumerate(NEAR):
        load(("row", i), row_hbm.at[level], rowf.at[pl.ds(RANK * i, RANK)])
    load("leaf", leaf_hbm, leaf)
    load("row0", row_hbm.at[0], row0)
    load("col0", col_hbm.at[0], col0)
    load("inc", inc_hbm, inc)
    for i, level in enumerate(NEAR + FAR):
        load(("col", i), col_hbm.at[level], colf.at[pl.ds(RANK * i, RANK)])
    load("inv", inv_hbm, inv)

    plus1, minus1 = (z + 1) % 8, (z + 7) % 8
    plus2, minus2 = (z + 2) % 8, (z + 6) % 8
    peers = [(other, z)]
    peers += [(wide, flip(z, m)) for m in range(1, 8)]
    peers += [(flip(plane, m) * 2 + core, z) for m in range(1, 16)]
    peers += [(other, k) for k in (plus1, minus1, plus2, minus2)]
    barrier = pltpu.get_barrier_semaphore()
    for peer in peers:
        pl.semaphore_signal(barrier, inc=1, device_id=peer, device_id_type=MESH)

    copies = []

    def send(turn, src, dst, device):
        index = len(copies)
        copy = pltpu.make_async_remote_copy(
            src_ref=src, dst_ref=dst, send_sem=send_sem.at[index], recv_sem=recv_sem.at[index],
            device_id=device, device_id_type=MESH)
        copy.start()
        copies.append(copy)
        return copy

    lane = lax.broadcasted_iota(jnp.int32, (8, 128), 1)
    slot = z % 4

    def exchange(turn, make_far, make_near, hidden, settle):
        near_t, far_t, swap_t, mine_t = near.at[turn], far.at[turn], swap.at[turn], mine.at[turn]
        ring_far_t, sum_far_t, cross_t = ring_far.at[turn], sum_far.at[turn], cross.at[turn]
        fin_far_t, all_far_t = fin_far.at[turn], all_far.at[turn]
        ring_near_t, fin_near_t, fin_four_t = ring_near.at[turn], fin_near.at[turn], fin_four.at[turn]
        all_near_t, all_four_t = all_near.at[turn], all_four.at[turn]

        far_t[...] = make_far()
        if turn == 0:
            pl.semaphore_wait(barrier, len(peers))
        theirs = pl.ds(pl.multiple_of(32 * (1 - core), 32), 32)
        ours = pl.ds(pl.multiple_of(32 * core, 32), 32)
        core_copy = send(turn, far_t.at[theirs], swap_t, (other, z))
        near_t[...] = make_near()
        core_copy.wait_recv()
        mine_t[...] = far_t[ours, :] + swap_t[...]

        far_ring = []
        for m in range(1, 8):
            dest = flip(z, m)
            rows = pl.ds(pl.multiple_of(8 * (dest % 4), 8), 8)
            far_ring.append(send(turn, mine_t.at[rows], ring_far_t.at[m], (wide, dest)))
        near_ring = []
        for m in range(1, 8):
            dest = flip(z, m)
            rows = pl.ds(pl.multiple_of(16 * (dest % 4), 16), 16)
            near_ring.append(send(turn, near_t.at[rows], ring_near_t.at[z], (wide, dest)))
        own16 = pl.ds(pl.multiple_of(16 * slot, 16), 16)
        own8 = pl.ds(pl.multiple_of(8 * slot, 8), 8)
        ring_near_t[z] = near_t[own16, :]

        hidden(0)

        for copy in far_ring:
            copy.wait_recv()
        total = mine_t[own8, :]
        for m in range(1, 8):
            total = total + ring_far_t[m]
        sum_far_t[...] = total

        plane_copies = []
        for m in sorted(range(1, 16), key=lambda m: -m):
            first, last = tiles_of(level_of(m))
            lanes = pl.ds(128 * first, 128 * (last - first))
            plane_copies.append(send(turn, sum_far_t.at[:, lanes], cross_t.at[m, :, lanes],
                                     (flip(plane, m) * 2 + core, z)))

        hidden(1)

        for copy in near_ring:
            copy.wait_recv()
        pair = [ring_near_t[2 * k] + ring_near_t[2 * k + 1] for k in range(4)]
        quad = [pair[0] + pair[1], pair[2] + pair[3]]
        lane16 = lax.broadcasted_iota(jnp.int32, (16, HALF), 1)
        readers = (z, plus1, minus1, plus2)
        for k, reader in enumerate(readers):
            one = ring_near_t[flip(reader, 1)]
            which = reader // 2
            two = jnp.where(which == 0, pair[1], jnp.where(which == 1, pair[0], jnp.where(which == 2, pair[3], pair[2])))
            three = jnp.where(reader // 4 == 0, quad[1], quad[0])
            fin_near_t[k] = jnp.where(lane16 < RANK, one, jnp.where(lane16 < 2 * RANK, two, three))
        fin_four_t[...] = (quad[0] + quad[1])[:, 256:]
        all_near_t[own16, :] = fin_near_t[0]
        near_same = [send(turn, fin_near_t.at[k], all_near_t.at[own16], (wide, readers[k])) for k in (1, 2, 3)]
        near_other = [send(turn, fin_four_t, all_four_t.at[own16], (other, readers[k])) for k in (0, 1, 2, 3)]

        for copy in plane_copies:
            copy.wait_recv()
        for tile in range(3):
            lanes = pl.ds(128 * tile, 128)
            value = jnp.zeros((8, 128), F32)
            for level in FAR:
                first, last = tiles_of(level)
                if not first <= tile < last:
                    continue
                part = None
                for m in range(1, 16):
                    if level_of(m) == level:
                        piece = cross_t[m, :, lanes]
                        part = piece if part is None else part + piece
                low = FAR_LANE[level] - 128 * tile
                inside = jnp.logical_and(lane >= low, lane < low + RANK)
                value = jnp.where(inside, part, value)
            fin_far_t[:, lanes] = value
        own_far = pl.ds(pl.multiple_of(32 * core + 8 * slot, 8), 8)
        all_far_t[own_far, :] = fin_far_t[...]
        far_gather = []
        for k in (3, 1, 2):
            far_gather.append(send(turn, fin_far_t, all_far_t.at[own_far], (wide, readers[k])))
            far_gather.append(send(turn, fin_far_t, all_far_t.at[own_far], (other, readers[k])))
        far_gather.append(send(turn, fin_far_t, all_far_t.at[own_far], (other, z)))

        for copy in near_same + near_other:
            copy.wait_recv()
        lane64 = lax.broadcasted_iota(jnp.int32, (COLS, 128), 1)
        last = jnp.where(lane64 < 32, all_near_t[:, 256:], all_four_t[...])
        coefs_near = jnp.concatenate([all_near_t[:, :256], last], axis=1)
        settle(0, coefs_near)
        for copy in far_gather:
            copy.wait_recv()
        settle(1, all_far_t[...])

    def far_part(stacked):
        return mul_t(stacked, row_h[HALF:, :], row_l[HALF:, :])

    def near_part(stacked):
        return mul_t(stacked, row_h[:HALF, :], row_l[:HALF, :])

    def local_image(stacked):
        coefs = []
        for h in range(2):
            cols = slice(LEAF * h, LEAF * (h + 1))
            coefs.append(stack_split(mul_t(stacked[:, cols], row0_h[:, cols], row0_l[:, cols])))
        parts = []
        for h in range(2):
            cols = slice(LEAF * h, LEAF * (h + 1))
            image = mul(stacked[:, cols], leaf_h[:, cols], leaf_l[:, cols])
            parts.append(image + mul(coefs[1 - h], col0_h[:, cols], col0_l[:, cols]))
        return jnp.concatenate(parts, axis=1)

    def far_image(group, coefs):
        rows = slice(HALF * group, HALF * (group + 1))
        return mul(stack_split(coefs), col_h[rows, :], col_l[rows, :])

    loads["sol"].wait()
    sol_s = stack_split(sol[...])

    def first_far():
        for i in range(4, 8):
            loads[("row", i)].wait()
        split_rows(rowf.at[pl.ds(HALF, HALF)], row_h.at[pl.ds(HALF, HALF)], row_l.at[pl.ds(HALF, HALF)])
        return far_part(sol_s)

    def first_near():
        for i in range(4):
            loads[("row", i)].wait()
        split_rows(rowf.at[pl.ds(0, HALF)], row_h.at[pl.ds(0, HALF)], row_l.at[pl.ds(0, HALF)])
        return near_part(sol_s)

    def first_hidden(stage):
        if stage == 0:
            for name in ("leaf", "row0", "col0", "inc"):
                loads[name].wait()
            split_rows(leaf, leaf_h, leaf_l)
            split_rows(row0, row0_h, row0_l)
            split_rows(col0, col0_h, col0_l)
            base[...] = inc[...] - local_image(sol_s)
        else:
            for i in range(8):
                loads[("col", i)].wait()
            split_rows(colf, col_h, col_l)
            loads["inv"].wait()
            split_rows(inv, inv_h, inv_l)

    def first_settle(group, coefs):
        base[...] = base[...] - far_image(group, coefs)

    exchange(0, first_far, first_near, first_hidden, first_settle)

    residual_s = stack_split(base[...])
    for h in range(2):
        cols = slice(LEAF * h, LEAF * (h + 1))
        refined[:, cols] = sol[:, cols] + mul(residual_s[:, cols], inv_h[:, cols], inv_l[:, cols])
    ref_copy = pltpu.make_async_copy(refined, ref_hbm, out_sem.at[0])
    ref_copy.start()
    refined_s = stack_split(refined[...])

    def second_hidden(stage):
        if stage == 0:
            out[...] = inc[...] - local_image(refined_s)

    def second_settle(group, coefs):
        out[...] = out[...] - far_image(group, coefs)

    exchange(1, lambda: far_part(refined_s), lambda: near_part(refined_s), second_hidden, second_settle)

    res_copy = pltpu.make_async_copy(out, res_hbm, out_sem.at[1])
    res_copy.start()
    for copy in copies:
        copy.wait_send()
    ref_copy.wait()
    res_copy.wait()


def per_device(solution, incident, leaf_blocks, leaf_inverse, col_basis, row_basis):
    vmem = pltpu.VMEM
    n_copies = 2 * (1 + 7 + 7 + 15 + 3 + 4 + 7)
    scratch = [
        vmem((COLS, ROWS), F32), vmem((COLS, ROWS), F32), vmem((LEAF, ROWS), F32), vmem((LEAF, ROWS), F32),
        vmem((2 * HALF, ROWS), F32), vmem((2 * HALF, ROWS), F32), vmem((RANK, ROWS), F32), vmem((RANK, ROWS), F32),
        vmem((LEAF, ROWS), BF16), vmem((LEAF, ROWS), BF16), vmem((LEAF, ROWS), BF16), vmem((LEAF, ROWS), BF16),
        vmem((2 * HALF, ROWS), BF16), vmem((2 * HALF, ROWS), BF16),
        vmem((2 * HALF, ROWS), BF16), vmem((2 * HALF, ROWS), BF16),
        vmem((RANK, ROWS), BF16), vmem((RANK, ROWS), BF16), vmem((RANK, ROWS), BF16), vmem((RANK, ROWS), BF16),
        vmem((COLS, ROWS), F32), vmem((COLS, ROWS), F32), vmem((COLS, ROWS), F32),
        vmem((2, COLS, HALF), F32),
        vmem((2, COLS, HALF), F32),
        vmem((2, 32, HALF), F32),
        vmem((2, 32, HALF), F32),
        vmem((2, 8, 8, HALF), F32),
        vmem((2, 8, HALF), F32),
        vmem((2, 16, 8, HALF), F32),
        vmem((2, 8, HALF), F32),
        vmem((2, COLS, HALF), F32),
        vmem((2, 8, 16, HALF), F32),
        vmem((2, 4, 16, HALF), F32),
        vmem((2, 16, 128), F32),
        vmem((2, COLS, HALF), F32),
        vmem((2, COLS, 128), F32),
        pltpu.SemaphoreType.DMA((24,)),
        pltpu.SemaphoreType.DMA((2,)),
        pltpu.SemaphoreType.DMA((n_copies,)),
        pltpu.SemaphoreType.DMA((n_copies,)),
    ]
    anywhere = pl.BlockSpec(memory_space=pl.ANY)
    shape = jax.ShapeDtypeStruct((COLS, ROWS), F32)
    return pl.pallas_call(
        kernel,
        out_shape=(shape, shape),
        in_specs=[anywhere] * 6,
        out_specs=(anywhere, anywhere),
        scratch_shapes=scratch,
        compiler_params=pltpu.CompilerParams(
            collective_id=0, has_side_effects=True, vmem_limit_bytes=60 * 1024 * 1024),
    )(solution, incident, leaf_blocks, leaf_inverse, col_basis, row_basis)


def solution(mesh):
    in_specs = (
        P(None, ("wide", "grp")),
        P(None, ("wide", "grp")),
        P(None, ("wide", "grp")),
        P(None, ("wide", "grp")),
        P(None, None, ("wide", "grp")),
        P(None, None, ("wide", "grp")),
    )
    out_specs = (P(None, ("wide", "grp")), P(None, ("wide", "grp")))
    return jax.shard_map(
        per_device, mesh=mesh, in_specs=in_specs, out_specs=out_specs, check_vma=False
    )
```

time: 138 us -> 52.8 us (0.38)
  the two profiles are of different devices: /device:TPU:16 before, /device:TPU:1 now
where the time goes in v1:
time: 52.8 us; the launch traced here: 52.7 us
  Pallas kernels  48.7 us (92%)
  local copies, waits for them, and re-layouts  3.34 us (6%)
  between operations  0.64 us (1%)
    pallas_call x1, Pallas kernels, per_device(): pl.pallas_call(kernel, out_shape=(shape, shape), in_specs=[anywhere] * 6,...  48.7 us
    unnamed x2, local copies, waits for them, and re-layouts  3.34 us

profile of v1, /device:TPU:1, one launch (start us, length us, event | category | flops | bytes accessed | tf_op | source)
XLA Modules:
  0.0 52.7 jit_solution(4699238399715558921)
XLA Ops:
  0.6 48.7 %shard_map.77 = (f32[64,1024]{1,0:T(8,128)}, f32[64,1024]{1,0:T(8,128)}) custom-call(f32[64,1024]{1,0:T(8,128)} %sol_hbm.1, f32[64,1024]{1,0:T(8,128)} %inc_hbm.1, f32[512,1024]{1,0:T(8,128)} %leaf_hbm.1, f32[512,1024]{1,0:T(8,128)} %inv_hbm.1, f32[9,96,1024]{2,1,0:T(8,128)} %col_hbm.1, f32[9,96,1024]{2,1,0:T(8,128)} %row_hbm.1), custom_call_target="tpu_custom_call" | custom-call | tf_op jit(solution)/shard_map/pallas_call | solution.py:344
  49.3 1.7 %copy.10 = f32[64,1024]{1,0:T(8,128)} copy(f32[64,1024]{1,0:T(8,128)} %get-tuple-element.4) | data formatting | bytes 524288
  51.0 1.7 %copy.11 = f32[64,1024]{1,0:T(8,128)} copy(f32[64,1024]{1,0:T(8,128)} %get-tuple-element.5) | data formatting | bytes 524288

commit v2 on v1

v2 whole, which is shorter than its diff:
```python
import functools

import jax
import jax.numpy as jnp
from jax import lax
from jax.experimental import pallas as pl
from jax.experimental.pallas import tpu as pltpu
from jax.sharding import PartitionSpec as P

MESH = pl.DeviceIdType.MESH
F32 = jnp.float32
BF16 = jnp.bfloat16
RANK = 96
COLS = 64
ROWS = 1024
LEAF = 512
HALF = 384
NEAR = (1, 2, 3, 4)
FAR = (8, 5, 6, 7)
FAR_LANE = {level: RANK * i for i, level in enumerate(FAR)}


def flip(value, mask):
    for bit in range(4):
        if mask >> bit & 1:
            value = value + (1 - 2 * ((value // (1 << bit)) % 2)) * (1 << bit)
    return value


RING = (4, 3, 5, 2, 6, 1, 7)
HOPS = (0, 1, 2, 1)
PLANE = tuple(sorted(range(1, 16), key=lambda m: -(HOPS[m % 4] + HOPS[m // 4])))
NEAR_PEERS = (4, 5, 6, 7, 2, 3, 1)


def near_level(mask):
    return mask.bit_length()


def level_of(mask):
    return 5 + mask.bit_length() - 1


def tiles_of(level):
    low = FAR_LANE[level]
    return low // 128, (low + RANK - 1) // 128 + 1


def split(value):
    high = value.astype(BF16)
    low = (value - high.astype(F32)).astype(BF16)
    return high, low


def split_rows(src, high_ref, low_ref, step=32):
    @pl.loop(0, src.shape[0] // step)
    def _(i):
        rows = pl.ds(pl.multiple_of(i * step, step), step)
        high, low = split(src[rows, :])
        high_ref[rows, :] = high
        low_ref[rows, :] = low


def stack_split(value):
    high, low = split(value)
    return jnp.concatenate([high, low], axis=0)


def mul(stacked, high, low):
    top = jnp.dot(stacked, high, preferred_element_type=F32)
    return top[:COLS] + top[COLS:] + jnp.dot(stacked[:COLS], low, preferred_element_type=F32)


def mul_t(stacked, high, low):
    dims = (((1,), (1,)), ((), ()))
    top = lax.dot_general(stacked, high, dims, preferred_element_type=F32)
    return top[:COLS] + top[COLS:] + lax.dot_general(stacked[:COLS], low, dims, preferred_element_type=F32)


def pack(value):
    lane = lax.broadcasted_iota(jnp.int32, (16, 128), 1)
    rest = value[48:]
    rows = [jnp.where(lane < RANK, value[16 * j:16 * j + 16], pltpu.roll(rest, RANK - 32 * j, 1)) for j in range(3)]
    return jnp.concatenate(rows, axis=0)


def unpack(value):
    lane = lax.broadcasted_iota(jnp.int32, (16, 128), 1)
    moved = [pltpu.roll(value[16 * j:16 * j + 16], 32 * j + 32, 1) for j in range(3)]
    rest = jnp.where(lane < 32, moved[0], jnp.where(lane < 64, moved[1], moved[2]))
    return jnp.concatenate([value, rest], axis=0)


def apart(dense):
    lane = lax.broadcasted_iota(jnp.int32, (COLS, 128), 1)
    t0, t1, t2 = dense[:, :128], dense[:, 128:256], dense[:, 256:]
    return (t0, pltpu.roll(jnp.where(lane >= 96, t0, t1), 32, 1),
            pltpu.roll(jnp.where(lane >= 64, t1, t2), 64, 1), pltpu.roll(t2, 96, 1))


def together(c1, c2, c3, c4):
    lane = lax.broadcasted_iota(jnp.int32, (COLS, 128), 1)
    c2, c3, c4 = pltpu.roll(c2, 96, 1), pltpu.roll(c3, 64, 1), pltpu.roll(c4, 32, 1)
    return jnp.concatenate(
        [jnp.where(lane < 96, c1, c2), jnp.where(lane < 64, c2, c3), jnp.where(lane < 32, c3, c4)], axis=1)


def kernel(sol_hbm, inc_hbm, leaf_hbm, inv_hbm, col_hbm, row_hbm, refined, out, *scratch):
    (sol, inc, leaf, inv, colf, rowf, col0, row0,
     leaf_h, leaf_l, inv_h, inv_l, col_h, col_l, row_h, row_l, col0_h, col0_l, row0_h, row0_l,
     mid_h, mid_l, map_h, map_l, base, ahead,
     near, four, far, swap, mine, ring_far, sum_far, cross, fin_far, all_far,
     near_in, ring_four, fin_four, all_four,
     in_sem, send_sem, recv_sem) = scratch

    wide = lax.axis_index("wide")
    z = lax.axis_index("grp")
    core = wide % 2
    plane = wide // 2
    other = wide + 1 - 2 * core

    plus1, minus1 = (z + 1) % 8, (z + 7) % 8
    plus2, minus2 = (z + 2) % 8, (z + 6) % 8
    peers = [(flip(plane, m) * 2 + core, z) for m in PLANE]
    peers += [(wide, (z + k) % 8) for k in RING]
    peers += [(other, k) for k in (plus2, minus2, plus1, minus1)]
    peers += [(other, z)]
    barrier = pltpu.get_barrier_semaphore()
    for peer in peers:
        pl.semaphore_signal(barrier, inc=1, device_id=peer, device_id_type=MESH)

    loads = {}

    def load(name, src, dst):
        copy = pltpu.make_async_copy(src, dst, in_sem.at[len(loads)])
        copy.start()
        loads[name] = copy

    load("sol", sol_hbm, sol)
    for i, level in enumerate(FAR):
        load(("row", i + 4), row_hbm.at[level], rowf.at[pl.ds(HALF + RANK * i, RANK)])
    for i, level in enumerate(NEAR):
        load(("row", i), row_hbm.at[level], rowf.at[pl.ds(RANK * i, RANK)])
    load("leaf", leaf_hbm, leaf)
    load("row0", row_hbm.at[0], row0)
    load("col0", col_hbm.at[0], col0)
    load("inc", inc_hbm, inc)
    load("inv", inv_hbm, inv)
    for i, level in enumerate(NEAR + FAR):
        load(("col", i), col_hbm.at[level], colf.at[pl.ds(RANK * i, RANK)])

    copies = []

    def send(src, dst, device):
        index = len(copies)
        copy = pltpu.make_async_remote_copy(
            src_ref=src, dst_ref=dst, send_sem=send_sem.at[index], recv_sem=recv_sem.at[index],
            device_id=device, device_id_type=MESH)
        copy.start()
        copies.append(copy)
        return copy

    lane = lax.broadcasted_iota(jnp.int32, (8, 128), 1)
    slot = z % 4
    beyond = (z + 2 + 4 * core) % 8
    readers = (beyond, plus1, minus1)

    def exchange(turn, make_far, during_core, make_near, hidden, settle):
        near_t, four_t, far_t, swap_t, mine_t = near.at[turn], four.at[turn], far.at[turn], swap.at[turn], mine.at[turn]
        ring_far_t, sum_far_t, cross_t = ring_far.at[turn], sum_far.at[turn], cross.at[turn]
        fin_far_t, all_far_t = fin_far.at[turn], all_far.at[turn]
        near_in_t, ring_four_t, fin_four_t, all_four_t = near_in.at[turn], ring_four.at[turn], fin_four.at[turn], all_four.at[turn]

        far_t[...] = make_far()
        if turn == 0:
            pl.semaphore_wait(barrier, len(peers))
        theirs = pl.ds(pl.multiple_of(32 * (1 - core), 32), 32)
        ours = pl.ds(pl.multiple_of(32 * core, 32), 32)
        core_copy = send(far_t.at[theirs], swap_t, (other, z))
        during_core()
        core_copy.wait_recv()
        mine_t[...] = far_t[ours, :] + swap_t[...]

        far_ring = []
        for k in RING:
            dest = (z + k) % 8
            rows = pl.ds(pl.multiple_of(8 * (dest % 4), 8), 8)
            far_ring.append(send(mine_t.at[rows], ring_far_t.at[k], (wide, dest)))

        levels = apart(make_near())
        four_t[...] = levels[3]
        for level in (1, 2, 3):
            near_t[level] = pack(levels[level - 1])
        four_ring = []
        for k in RING:
            dest = (z + k) % 8
            rows = pl.ds(pl.multiple_of(16 * (dest % 4), 16), 16)
            four_ring.append(send(four_t.at[rows], ring_four_t.at[k], (wide, dest)))
        near_copies = []
        for m in NEAR_PEERS:
            near_copies.append(send(near_t.at[near_level(m)], near_in_t.at[m], (wide, flip(z, m))))

        hidden(0)

        own16 = pl.ds(pl.multiple_of(16 * slot, 16), 16)
        own8 = pl.ds(pl.multiple_of(8 * slot, 8), 8)
        for copy in far_ring:
            copy.wait_recv()
        total = mine_t[own8, :]
        for k in range(1, 8):
            total = total + ring_far_t[k]
        sum_far_t[...] = total

        plane_copies = []
        for m in PLANE:
            first, last = tiles_of(level_of(m))
            lanes = pl.ds(128 * first, 128 * (last - first))
            plane_copies.append(send(sum_far_t.at[:, lanes], cross_t.at[m, :, lanes],
                                     (flip(plane, m) * 2 + core, z)))

        for copy in four_ring:
            copy.wait_recv()
        total = four_t[own16, :]
        for k in range(1, 8):
            total = total + ring_four_t[k]
        fin_four_t[...] = total
        four_gather = [send(fin_four_t, all_four_t.at[own16], (other, reader)) for reader in readers]
        four_gather.append(send(fin_four_t, all_four_t.at[own16], (other, z)))

        hidden(1)

        for copy in plane_copies:
            copy.wait_recv()
        for tile in range(3):
            lanes = pl.ds(128 * tile, 128)
            value = jnp.zeros((8, 128), F32)
            for level in FAR:
                first, last = tiles_of(level)
                if not first <= tile < last:
                    continue
                part = None
                for m in range(1, 16):
                    if level_of(m) == level:
                        piece = cross_t[m, :, lanes]
                        part = piece if part is None else part + piece
                low = FAR_LANE[level] - 128 * tile
                inside = jnp.logical_and(lane >= low, lane < low + RANK)
                value = jnp.where(inside, part, value)
            fin_far_t[:, lanes] = value
        own_far = pl.ds(pl.multiple_of(32 * core + 8 * slot, 8), 8)
        far_gather = []
        for reader in readers:
            far_gather.append(send(fin_far_t, all_far_t.at[own_far], (wide, reader)))
            far_gather.append(send(fin_far_t, all_far_t.at[own_far], (other, reader)))
        far_gather.append(send(fin_far_t, all_far_t.at[own_far], (other, z)))
        all_far_t[own_far, :] = fin_far_t[...]

        for copy in near_copies + four_gather:
            copy.wait_recv()
        c1 = unpack(near_in_t[1])
        c2 = unpack(near_in_t[2] + near_in_t[3])
        c3 = unpack((near_in_t[4] + near_in_t[5]) + (near_in_t[6] + near_in_t[7]))
        settle(0, together(c1, c2, c3, all_four_t[...]))
        for copy in far_gather:
            copy.wait_recv()
        settle(1, all_far_t[...])

    def far_part(stacked):
        return mul_t(stacked, row_h[HALF:, :], row_l[HALF:, :])

    def near_part(stacked):
        return mul_t(stacked, row_h[:HALF, :], row_l[:HALF, :])

    def local_image(stacked):
        coefs = []
        for h in range(2):
            cols = slice(LEAF * h, LEAF * (h + 1))
            coefs.append(stack_split(mul_t(stacked[:, cols], row0_h[:, cols], row0_l[:, cols])))
        parts = []
        for h in range(2):
            cols = slice(LEAF * h, LEAF * (h + 1))
            image = mul(stacked[:, cols], leaf_h[:, cols], leaf_l[:, cols])
            parts.append(image + mul(coefs[1 - h], col0_h[:, cols], col0_l[:, cols]))
        return jnp.concatenate(parts, axis=1)

    def far_image(group, coefs):
        rows = slice(HALF * group, HALF * (group + 1))
        return mul(stack_split(coefs), col_h[rows, :], col_l[rows, :])

    def refine():
        residual_s = stack_split(base[...])
        parts = []
        for h in range(2):
            cols = slice(LEAF * h, LEAF * (h + 1))
            parts.append(sol[:, cols] + mul(residual_s[:, cols], inv_h[:, cols], inv_l[:, cols]))
        return jnp.concatenate(parts, axis=1)

    loads["sol"].wait()
    sol_s = stack_split(sol[...])

    def first_far():
        for i in range(4, 8):
            loads[("row", i)].wait()
        split_rows(rowf.at[pl.ds(HALF, HALF)], row_h.at[pl.ds(HALF, HALF)], row_l.at[pl.ds(HALF, HALF)])
        return far_part(sol_s)

    near_value = []

    def first_during():
        for i in range(4):
            loads[("row", i)].wait()
        split_rows(rowf.at[pl.ds(0, HALF)], row_h.at[pl.ds(0, HALF)], row_l.at[pl.ds(0, HALF)])
        near_value.append(near_part(sol_s))

    def first_hidden(stage):
        if stage == 0:
            for name in ("leaf", "row0", "col0", "inc"):
                loads[name].wait()
            split_rows(leaf, leaf_h, leaf_l)
            split_rows(row0, row0_h, row0_l)
            split_rows(col0, col0_h, col0_l)
            base[...] = inc[...] - local_image(sol_s)
            loads["inv"].wait()
            split_rows(inv, inv_h, inv_l)
            for i in range(8):
                loads[("col", i)].wait()
            split_rows(colf, col_h, col_l)
            for h in range(2):
                for n in range(2):
                    rows = slice(LEAF * h, LEAF * (h + 1))
                    cols = slice(LEAF * h + 256 * n, LEAF * h + 256 * (n + 1))
                    value = jnp.dot(col_h[HALF:, rows], inv_h[:, cols], preferred_element_type=F32)
                    value = value + jnp.dot(col_l[HALF:, rows], inv_h[:, cols], preferred_element_type=F32)
                    value = value + jnp.dot(col_h[HALF:, rows], inv_l[:, cols], preferred_element_type=F32)
                    high, low = split(value)
                    mid_h[:, cols] = high
                    mid_l[:, cols] = low
        else:
            dims = (((1,), (1,)), ((), ()))
            for n in range(3):
                cols = slice(128 * n, 128 * (n + 1))
                rows = slice(HALF + 128 * n, HALF + 128 * (n + 1))
                value = lax.dot_general(mid_h[...], row_h[rows, :], dims, preferred_element_type=F32)
                value = value + lax.dot_general(mid_l[...], row_h[rows, :], dims, preferred_element_type=F32)
                value = value + lax.dot_general(mid_h[...], row_l[rows, :], dims, preferred_element_type=F32)
                high, low = split(value)
                map_h[:, cols] = high
                map_l[:, cols] = low

    coefs_far = []

    def first_settle(group, coefs):
        if group == 0:
            base[...] = base[...] - far_image(0, coefs)
            ahead[...] = far_part(stack_split(refine()))
        else:
            coefs_far.append(stack_split(coefs))

    exchange(0, first_far, first_during, lambda: near_value[0], first_hidden, first_settle)

    def second_far():
        return ahead[...] - mul(coefs_far[0], map_h[...], map_l[...])

    def second_during():
        base[...] = base[...] - mul(coefs_far[0], col_h[HALF:, :], col_l[HALF:, :])
        refined[...] = refine()

    def second_near():
        return near_part(stack_split(refined[...]))

    def second_hidden(stage):
        if stage == 0:
            out[...] = inc[...] - local_image(stack_split(refined[...]))

    def second_settle(group, coefs):
        out[...] = out[...] - far_image(group, coefs)

    exchange(1, second_far, second_during, second_near, second_hidden, second_settle)

    for copy in copies:
        copy.wait_send()


def per_device(solution, incident, leaf_blocks, leaf_inverse, col_basis, row_basis):
    vmem = pltpu.VMEM
    n_copies = 2 * (1 + 7 + 7 + 7 + 15 + 4 + 7)
    scratch = [
        vmem((COLS, ROWS), F32), vmem((COLS, ROWS), F32), vmem((LEAF, ROWS), F32), vmem((LEAF, ROWS), F32),
        vmem((2 * HALF, ROWS), F32), vmem((2 * HALF, ROWS), F32), vmem((RANK, ROWS), F32), vmem((RANK, ROWS), F32),
        vmem((LEAF, ROWS), BF16), vmem((LEAF, ROWS), BF16), vmem((LEAF, ROWS), BF16), vmem((LEAF, ROWS), BF16),
        vmem((2 * HALF, ROWS), BF16), vmem((2 * HALF, ROWS), BF16),
        vmem((2 * HALF, ROWS), BF16), vmem((2 * HALF, ROWS), BF16),
        vmem((RANK, ROWS), BF16), vmem((RANK, ROWS), BF16), vmem((RANK, ROWS), BF16), vmem((RANK, ROWS), BF16),
        vmem((HALF, ROWS), BF16), vmem((HALF, ROWS), BF16),
        vmem((HALF, HALF), BF16), vmem((HALF, HALF), BF16),
        vmem((COLS, ROWS), F32),
        vmem((COLS, HALF), F32),
        vmem((2, 4, 48, 128), F32),
        vmem((2, COLS, 128), F32),
        vmem((2, COLS, HALF), F32),
        vmem((2, 32, HALF), F32),
        vmem((2, 32, HALF), F32),
        vmem((2, 8, 8, HALF), F32),
        vmem((2, 8, HALF), F32),
        vmem((2, 16, 8, HALF), F32),
        vmem((2, 8, HALF), F32),
        vmem((2, COLS, HALF), F32),
        vmem((2, 8, 48, 128), F32),
        vmem((2, 8, 16, 128), F32),
        vmem((2, 16, 128), F32),
        vmem((2, COLS, 128), F32),
        pltpu.SemaphoreType.DMA((24,)),
        pltpu.SemaphoreType.DMA((n_copies,)),
        pltpu.SemaphoreType.DMA((n_copies,)),
    ]
    anywhere = pl.BlockSpec(memory_space=pltpu.HBM)
    resident = pl.BlockSpec(memory_space=pltpu.VMEM)
    shape = jax.ShapeDtypeStruct((COLS, ROWS), F32)
    return pl.pallas_call(
        kernel,
        out_shape=(shape, shape),
        in_specs=[anywhere] * 6,
        out_specs=(resident, resident),
        scratch_shapes=scratch,
        compiler_params=pltpu.CompilerParams(
            collective_id=0, has_side_effects=True, vmem_limit_bytes=36 * 1024 * 1024),
    )(*(pltpu.with_memory_space_constraint(x, pltpu.HBM) for x in (
        solution, incident, leaf_blocks, leaf_inverse, col_basis, row_basis)))


def solution(mesh):
    in_specs = (
        P(None, ("wide", "grp")),
        P(None, ("wide", "grp")),
        P(None, ("wide", "grp")),
        P(None, ("wide", "grp")),
        P(None, None, ("wide", "grp")),
        P(None, None, ("wide", "grp")),
    )
    out_specs = (P(None, ("wide", "grp")), P(None, ("wide", "grp")))
    return jax.shard_map(
        per_device, mesh=mesh, in_specs=in_specs, out_specs=out_specs, check_vma=False
    )
```

time: 52.8 us -> 46.3 us (0.88)
  Pallas kernels: 48.7 us -> 44.2 us
  local copies, waits for them, and re-layouts: 3.34 us -> 1.41 us
    pallas_call x1, Pallas kernels: 48.7 us -> 44.2 us  [per_device(): pl.pallas_call(kernel, out_shape=(shape, shape), in_specs=[anywhere] * 6,...]
    unnamed x2, local copies, waits for them, and re-layouts: 3.34 us -> 1.41 us
where the time goes in v2:
time: 46.3 us; the launch traced here: 46.2 us
  Pallas kernels  44.2 us (95%)
  local copies, waits for them, and re-layouts  1.41 us (3%)
  between operations  0.64 us (1%)
    pallas_call x1, Pallas kernels, per_device(): pl.pallas_call(kernel, out_shape=(shape, shape), in_specs=[anywhere] * 6,...  44.2 us
    unnamed x2, local copies, waits for them, and re-layouts  1.41 us

profile of v2, /device:TPU:1, one launch (start us, length us, event | category | flops | bytes accessed | tf_op | source)
XLA Modules:
  0.0 46.2 jit_solution(4564936003815612592)
XLA Ops:
  0.6 44.2 %shard_map.77 = (f32[64,1024]{1,0:T(8,128)S(1)}, f32[64,1024]{1,0:T(8,128)S(1)}) custom-call(f32[64,1024]{1,0:T(8,128)} %sol_hbm.1, f32[64,1024]{1,0:T(8,128)} %inc_hbm.1, f32[512,1024]{1,0:T(8,128)} %leaf_hbm.1, f32[512,1024]{1,0:T(8,128)} %inv_hbm.1, f32[9,96,1024]{2,1,0:T(8,128)} %col_hbm.1, f32[9,96,1024]{2,1,0:T(8,128)} %row_hbm.1), custom_call_target="tpu_custom_call" | custom-call | tf_op jit(solution)/shard_map/pallas_call | solution.py:419
  44.8 0.7 %copy.10 = f32[64,1024]{1,0:T(8,128)} copy(f32[64,1024]{1,0:T(8,128)S(1)} %get-tuple-element.4) | data formatting | bytes 524288
  45.5 0.7 %copy.11 = f32[64,1024]{1,0:T(8,128)} copy(f32[64,1024]{1,0:T(8,128)S(1)} %get-tuple-element.5) | data formatting | bytes 524288

commit v3 on v2

--- a/solution.py
+++ b/solution.py
@@ -46,19 +46,22 @@
     return low // 128, (low + RANK - 1) // 128 + 1
 
 
+CROSS = tuple((m, tile) for m in PLANE for tile in range(*tiles_of(level_of(m))))
+
+
 def split(value):
     high = value.astype(BF16)
     low = (value - high.astype(F32)).astype(BF16)
     return high, low
 
 
-def split_rows(src, high_ref, low_ref, step=32):
+def split_rows(src, high_ref, low_ref, step=32, cols=slice(None)):
     @pl.loop(0, src.shape[0] // step)
     def _(i):
         rows = pl.ds(pl.multiple_of(i * step, step), step)
-        high, low = split(src[rows, :])
-        high_ref[rows, :] = high
-        low_ref[rows, :] = low
+        high, low = split(src[rows, cols])
+        high_ref[rows, cols] = high
+        low_ref[rows, cols] = low
 
 
 def stack_split(value):
@@ -119,46 +122,61 @@
     plane = wide // 2
     other = wide + 1 - 2 * core
 
+    names = []
+
+    def load(name, pairs, whole):
+        sem = in_sem.at[len(names)]
+        names.append(name)
+        for src, dst in pairs:
+            pltpu.make_async_copy(src, dst, sem).start()
+        loads[name] = pltpu.make_async_copy(whole, whole, sem)
+
+    loads = {}
+    load("sol", [(sol_hbm, sol)], sol)
+    for h in range(2):
+        cols = pl.ds(LEAF * h, LEAF)
+        load(("far", h), [(row_hbm.at[level, :, cols], rowf.at[pl.ds(HALF + RANK * i, RANK), cols])
+                          for i, level in enumerate(FAR)], rowf.at[pl.ds(HALF, HALF), cols])
+
     plus1, minus1 = (z + 1) % 8, (z + 7) % 8
     plus2, minus2 = (z + 2) % 8, (z + 6) % 8
     peers = [(flip(plane, m) * 2 + core, z) for m in PLANE]
     peers += [(wide, (z + k) % 8) for k in RING]
     peers += [(other, k) for k in (plus2, minus2, plus1, minus1)]
     peers += [(other, z)]
+    peers = peers[:1] + peers[15:18] + peers[1:15] + peers[18:]
     barrier = pltpu.get_barrier_semaphore()
     for peer in peers:
         pl.semaphore_signal(barrier, inc=1, device_id=peer, device_id_type=MESH)
 
-    loads = {}
-
-    def load(name, src, dst):
-        copy = pltpu.make_async_copy(src, dst, in_sem.at[len(loads)])
-        copy.start()
-        loads[name] = copy
-
-    load("sol", sol_hbm, sol)
-    for i, level in enumerate(FAR):
-        load(("row", i + 4), row_hbm.at[level], rowf.at[pl.ds(HALF + RANK * i, RANK)])
-    for i, level in enumerate(NEAR):
-        load(("row", i), row_hbm.at[level], rowf.at[pl.ds(RANK * i, RANK)])
-    load("leaf", leaf_hbm, leaf)
-    load("row0", row_hbm.at[0], row0)
-    load("col0", col_hbm.at[0], col0)
-    load("inc", inc_hbm, inc)
-    load("inv", inv_hbm, inv)
-    for i, level in enumerate(NEAR + FAR):
-        load(("col", i), col_hbm.at[level], colf.at[pl.ds(RANK * i, RANK)])
-
-    copies = []
-
-    def send(src, dst, device):
-        index = len(copies)
-        copy = pltpu.make_async_remote_copy(
-            src_ref=src, dst_ref=dst, send_sem=send_sem.at[index], recv_sem=recv_sem.at[index],
-            device_id=device, device_id_type=MESH)
-        copy.start()
-        copies.append(copy)
-        return copy
+    load("near", [(row_hbm.at[level], rowf.at[pl.ds(RANK * i, RANK)]) for i, level in enumerate(NEAR)],
+         rowf.at[pl.ds(0, HALF)])
+    load("leaf", [(leaf_hbm, leaf)], leaf)
+    load("row0", [(row_hbm.at[0], row0)], row0)
+    load("col0", [(col_hbm.at[0], col0)], col0)
+    load("inc", [(inc_hbm, inc)], inc)
+    load("inv", [(inv_hbm, inv)], inv)
+    load("col", [(col_hbm.at[level], colf.at[pl.ds(RANK * i, RANK)]) for i, level in enumerate(NEAR + FAR)], colf)
+
+    groups = []
+
+    class Group:
+        def __init__(self, whole):
+            self.send_sem = send_sem.at[len(groups)]
+            self.recv_sem = recv_sem.at[len(groups)]
+            self.whole = whole
+            groups.append(self)
+
+        def send(self, src, dst, device):
+            pltpu.make_async_remote_copy(
+                src_ref=src, dst_ref=dst, send_sem=self.send_sem, recv_sem=self.recv_sem,
+                device_id=device, device_id_type=MESH).start()
+
+        def wait_recv(self):
+            pltpu.make_async_copy(self.whole, self.whole, self.recv_sem).wait()
+
+        def wait_send(self):
+            pltpu.make_async_copy(self.whole, self.whole, self.send_sem).wait()
 
     lane = lax.broadcasted_iota(jnp.int32, (8, 128), 1)
     slot = z % 4
@@ -176,61 +194,57 @@
             pl.semaphore_wait(barrier, len(peers))
         theirs = pl.ds(pl.multiple_of(32 * (1 - core), 32), 32)
         ours = pl.ds(pl.multiple_of(32 * core, 32), 32)
-        core_copy = send(far_t.at[theirs], swap_t, (other, z))
+        core_copy = Group(swap_t)
+        core_copy.send(far_t.at[theirs], swap_t, (other, z))
         during_core()
         core_copy.wait_recv()
         mine_t[...] = far_t[ours, :] + swap_t[...]
 
-        far_ring = []
+        far_ring = Group(ring_far_t.at[pl.ds(1, 7)])
         for k in RING:
             dest = (z + k) % 8
             rows = pl.ds(pl.multiple_of(8 * (dest % 4), 8), 8)
-            far_ring.append(send(mine_t.at[rows], ring_far_t.at[k], (wide, dest)))
+            far_ring.send(mine_t.at[rows], ring_far_t.at[k], (wide, dest))
 
         levels = apart(make_near())
         four_t[...] = levels[3]
         for level in (1, 2, 3):
             near_t[level] = pack(levels[level - 1])
-        four_ring = []
+        four_ring = Group(ring_four_t.at[pl.ds(1, 7)])
         for k in RING:
             dest = (z + k) % 8
             rows = pl.ds(pl.multiple_of(16 * (dest % 4), 16), 16)
-            four_ring.append(send(four_t.at[rows], ring_four_t.at[k], (wide, dest)))
-        near_copies = []
+            four_ring.send(four_t.at[rows], ring_four_t.at[k], (wide, dest))
+        near_copies = Group(near_in_t.at[pl.ds(1, 7)])
         for m in NEAR_PEERS:
-            near_copies.append(send(near_t.at[near_level(m)], near_in_t.at[m], (wide, flip(z, m))))
+            near_copies.send(near_t.at[near_level(m)], near_in_t.at[m], (wide, flip(z, m)))
 
         hidden(0)
 
         own16 = pl.ds(pl.multiple_of(16 * slot, 16), 16)
         own8 = pl.ds(pl.multiple_of(8 * slot, 8), 8)
-        for copy in far_ring:
-            copy.wait_recv()
+        far_ring.wait_recv()
         total = mine_t[own8, :]
         for k in range(1, 8):
             total = total + ring_far_t[k]
         sum_far_t[...] = total
 
-        plane_copies = []
-        for m in PLANE:
-            first, last = tiles_of(level_of(m))
-            lanes = pl.ds(128 * first, 128 * (last - first))
-            plane_copies.append(send(sum_far_t.at[:, lanes], cross_t.at[m, :, lanes],
-                                     (flip(plane, m) * 2 + core, z)))
-
-        for copy in four_ring:
-            copy.wait_recv()
+        plane_copies = Group(cross_t)
+        for index, (m, tile) in enumerate(CROSS):
+            plane_copies.send(sum_far_t.at[:, pl.ds(128 * tile, 128)], cross_t.at[index], (flip(plane, m) * 2 + core, z))
+
+        four_ring.wait_recv()
         total = four_t[own16, :]
         for k in range(1, 8):
             total = total + ring_four_t[k]
         fin_four_t[...] = total
-        four_gather = [send(fin_four_t, all_four_t.at[own16], (other, reader)) for reader in readers]
-        four_gather.append(send(fin_four_t, all_four_t.at[own16], (other, z)))
+        four_gather = Group(all_four_t)
+        for reader in readers + (z,):
+            four_gather.send(fin_four_t, all_four_t.at[own16], (other, reader))
 
         hidden(1)
 
-        for copy in plane_copies:
-            copy.wait_recv()
+        plane_copies.wait_recv()
         for tile in range(3):
             lanes = pl.ds(128 * tile, 128)
             value = jnp.zeros((8, 128), F32)
@@ -241,28 +255,27 @@
                 part = None
                 for m in range(1, 16):
                     if level_of(m) == level:
-                        piece = cross_t[m, :, lanes]
+                        piece = cross_t[CROSS.index((m, tile))]
                         part = piece if part is None else part + piece
                 low = FAR_LANE[level] - 128 * tile
                 inside = jnp.logical_and(lane >= low, lane < low + RANK)
                 value = jnp.where(inside, part, value)
             fin_far_t[:, lanes] = value
         own_far = pl.ds(pl.multiple_of(32 * core + 8 * slot, 8), 8)
-        far_gather = []
+        far_gather = Group(all_far_t.at[pl.ds(0, 56)])
         for reader in readers:
-            far_gather.append(send(fin_far_t, all_far_t.at[own_far], (wide, reader)))
-            far_gather.append(send(fin_far_t, all_far_t.at[own_far], (other, reader)))
-        far_gather.append(send(fin_far_t, all_far_t.at[own_far], (other, z)))
+            far_gather.send(fin_far_t, all_far_t.at[own_far], (wide, reader))
+            far_gather.send(fin_far_t, all_far_t.at[own_far], (other, reader))
+        far_gather.send(fin_far_t, all_far_t.at[own_far], (other, z))
         all_far_t[own_far, :] = fin_far_t[...]
 
-        for copy in near_copies + four_gather:
-            copy.wait_recv()
+        near_copies.wait_recv()
+        four_gather.wait_recv()
         c1 = unpack(near_in_t[1])
         c2 = unpack(near_in_t[2] + near_in_t[3])
         c3 = unpack((near_in_t[4] + near_in_t[5]) + (near_in_t[6] + near_in_t[7]))
         settle(0, together(c1, c2, c3, all_four_t[...]))
-        for copy in far_gather:
-            copy.wait_recv()
+        far_gather.wait_recv()
         settle(1, all_far_t[...])
 
     def far_part(stacked):
@@ -299,16 +312,18 @@
     sol_s = stack_split(sol[...])
 
     def first_far():
-        for i in range(4, 8):
-            loads[("row", i)].wait()
-        split_rows(rowf.at[pl.ds(HALF, HALF)], row_h.at[pl.ds(HALF, HALF)], row_l.at[pl.ds(HALF, HALF)])
-        return far_part(sol_s)
+        parts = []
+        for h in range(2):
+            loads[("far", h)].wait()
+            cols = slice(LEAF * h, LEAF * (h + 1))
+            split_rows(rowf.at[pl.ds(HALF, HALF)], row_h.at[pl.ds(HALF, HALF)], row_l.at[pl.ds(HALF, HALF)], cols=cols)
+            parts.append(mul_t(sol_s[:, cols], row_h[HALF:, cols], row_l[HALF:, cols]))
+        return parts[0] + parts[1]
 
     near_value = []
 
     def first_during():
-        for i in range(4):
-            loads[("row", i)].wait()
+        loads["near"].wait()
         split_rows(rowf.at[pl.ds(0, HALF)], row_h.at[pl.ds(0, HALF)], row_l.at[pl.ds(0, HALF)])
         near_value.append(near_part(sol_s))
 
@@ -322,8 +337,7 @@
             base[...] = inc[...] - local_image(sol_s)
             loads["inv"].wait()
             split_rows(inv, inv_h, inv_l)
-            for i in range(8):
-                loads[("col", i)].wait()
+            loads["col"].wait()
             split_rows(colf, col_h, col_l)
             for h in range(2):
                 for n in range(2):
@@ -337,9 +351,9 @@
                     mid_l[:, cols] = low
         else:
             dims = (((1,), (1,)), ((), ()))
-            for n in range(3):
-                cols = slice(128 * n, 128 * (n + 1))
-                rows = slice(HALF + 128 * n, HALF + 128 * (n + 1))
+            for low, high in ((0, 256), (256, 384)):
+                cols = slice(low, high)
+                rows = slice(HALF + low, HALF + high)
                 value = lax.dot_general(mid_h[...], row_h[rows, :], dims, preferred_element_type=F32)
                 value = value + lax.dot_general(mid_l[...], row_h[rows, :], dims, preferred_element_type=F32)
                 value = value + lax.dot_general(mid_h[...], row_l[rows, :], dims, preferred_element_type=F32)
@@ -377,13 +391,20 @@
 
     exchange(1, second_far, second_during, second_near, second_hidden, second_settle)
 
+    for group in groups:
+        group.wait_send()
+
+
+def finish(refined, out, refined_hbm, out_hbm, sem):
+    copies = [pltpu.make_async_copy(refined, refined_hbm, sem.at[0]), pltpu.make_async_copy(out, out_hbm, sem.at[1])]
     for copy in copies:
-        copy.wait_send()
+        copy.start()
+    for copy in copies:
+        copy.wait()
 
 
 def per_device(solution, incident, leaf_blocks, leaf_inverse, col_basis, row_basis):
     vmem = pltpu.VMEM
-    n_copies = 2 * (1 + 7 + 7 + 7 + 15 + 4 + 7)
     scratch = [
         vmem((COLS, ROWS), F32), vmem((COLS, ROWS), F32), vmem((LEAF, ROWS), F32), vmem((LEAF, ROWS), F32),
         vmem((2 * HALF, ROWS), F32), vmem((2 * HALF, ROWS), F32), vmem((RANK, ROWS), F32), vmem((RANK, ROWS), F32),
@@ -402,21 +423,21 @@
         vmem((2, 32, HALF), F32),
         vmem((2, 8, 8, HALF), F32),
         vmem((2, 8, HALF), F32),
-        vmem((2, 16, 8, HALF), F32),
+        vmem((2, len(CROSS), 8, 128), F32),
         vmem((2, 8, HALF), F32),
         vmem((2, COLS, HALF), F32),
         vmem((2, 8, 48, 128), F32),
         vmem((2, 8, 16, 128), F32),
         vmem((2, 16, 128), F32),
         vmem((2, COLS, 128), F32),
-        pltpu.SemaphoreType.DMA((24,)),
-        pltpu.SemaphoreType.DMA((n_copies,)),
-        pltpu.SemaphoreType.DMA((n_copies,)),
+        pltpu.SemaphoreType.DMA((10,)),
+        pltpu.SemaphoreType.DMA((14,)),
+        pltpu.SemaphoreType.DMA((14,)),
     ]
     anywhere = pl.BlockSpec(memory_space=pltpu.HBM)
     resident = pl.BlockSpec(memory_space=pltpu.VMEM)
     shape = jax.ShapeDtypeStruct((COLS, ROWS), F32)
-    return pl.pallas_call(
+    results = pl.pallas_call(
         kernel,
         out_shape=(shape, shape),
         in_specs=[anywhere] * 6,
@@ -426,6 +447,14 @@
             collective_id=0, has_side_effects=True, vmem_limit_bytes=36 * 1024 * 1024),
     )(*(pltpu.with_memory_space_constraint(x, pltpu.HBM) for x in (
         solution, incident, leaf_blocks, leaf_inverse, col_basis, row_basis)))
+    return pl.pallas_call(
+        finish,
+        out_shape=(shape, shape),
+        in_specs=[resident, resident],
+        out_specs=(anywhere, anywhere),
+        scratch_shapes=[pltpu.SemaphoreType.DMA((2,))],
+        compiler_params=pltpu.CompilerParams(vmem_limit_bytes=4 * 1024 * 1024),
+    )(*results)
 
 
 def solution(mesh):

time: 46.3 us -> 43.4 us (0.937)
  Pallas kernels: 44.2 us -> 42.7 us
  local copies, waits for them, and re-layouts: 1.41 us -> 0 us
    pallas_call x1, Pallas kernels: 44.2 us -> 41.9 us  [per_device(): pl.pallas_call(kernel, out_shape=(shape, shape), in_specs=[anywhere] * 6,...]
    unnamed x2 -> x0, local copies, waits for them, and re-layouts: 1.41 us -> none
    pallas_call x0 -> x1, Pallas kernels: none -> 0.81 us  [per_device(): pl.pallas_call(finish, out_shape=(shape, shape), in_specs=[resident, resi...]
where the time goes in v3:
time: 43.4 us; the launch traced here: 43.3 us
  Pallas kernels  42.7 us (98%)
  between operations  0.64 us (1%)
    pallas_call x1, Pallas kernels, per_device(): pl.pallas_call(kernel, out_shape=(shape, shape), in_specs=[anywhere] * 6,...  41.9 us

profile of v3, /device:TPU:1, one launch (start us, length us, event | category | flops | bytes accessed | tf_op | source)
XLA Modules:
  0.0 43.3 jit_solution(4043504922354270941)
XLA Ops:
  0.6 41.9 %shard_map.77 = (f32[64,1024]{1,0:T(8,128)S(1)}, f32[64,1024]{1,0:T(8,128)S(1)}) custom-call(f32[64,1024]{1,0:T(8,128)} %sol_hbm.1, f32[64,1024]{1,0:T(8,128)} %inc_hbm.1, f32[512,1024]{1,0:T(8,128)} %leaf_hbm.1, f32[512,1024]{1,0:T(8,128)} %inv_hbm.1, f32[9,96,1024]{2,1,0:T(8,128)} %col_hbm.1, f32[9,96,1024]{2,1,0:T(8,128)} %row_hbm.1), custom_call_target="tpu_custom_call" | custom-call | tf_op jit(solution)/shard_map/pallas_call | solution.py:440
  42.5 0.8 %shard_map.78 = (f32[64,1024]{1,0:T(8,128)}, f32[64,1024]{1,0:T(8,128)}) custom-call(f32[64,1024]{1,0:T(8,128)S(1)} %get-tuple-element.4.refined, f32[64,1024]{1,0:T(8,128)S(1)} %get-tuple-element.5.out), custom_call_target="tpu_custom_call" | custom-call | tf_op jit(solution)/shard_map/pallas_call | solution.py:450
